TPU v7x, 32 devices: a whole 2x2x4 slice. The times are simulated.
32 devices in a mesh: res: 4 (over x, core), blk: 8 (over z, y).
Axes of the slice: x: 2, y: 2, z: 4, core: 2. Of those that a mesh axis runs over, the one named last changes fastest.
Arguments:
- modes: float32 [2, 8, 4194304], P(None, 'res', 'blk'), may hold values from -0.078125 to 0.078125
Outputs:
- product_modes: float32 [2, 8, 4194304], P(None, 'res', 'blk')
All inputs are finite; a program needn't handle non-finite values.
Results may differ from a plain program's by a relative error of at most 0.000098.
Values sent between devices are 32-bit elements; how exact they have to be, the bound alone decides.
No kernel may reach another device: no remote copies, remote signals or barrier semaphores. Data moves between devices by JAX's collectives and lax.ppermute only.
A program may use at most 192 MiB of HBM per device.

v0:
```python
import math
import jax
import jax.numpy as jnp
from jax import lax
from jax.sharding import PartitionSpec as P

AXES = ("res", "blk")
PARTS = 12
KEPT = 8
SKIP = 4
high = lax.Precision.HIGH


def iota(shape, axis):
    return lax.broadcasted_iota(jnp.int32, shape, axis)


def unit(position, period):
    angle = 2.0 * math.pi / period * (position % period).astype(jnp.float32)
    return (jnp.cos(angle), jnp.sin(angle))


def cmul(left, right):
    return (left[0] * right[0] - left[1] * right[1], left[0] * right[1] + left[1] * right[0])


def real_form(pair, sign, axes=(0, 2)):
    c, s = pair
    s = sign * s
    return jnp.stack([jnp.stack([c, -s], axes[1] - 1), jnp.stack([s, c], axes[1] - 1)], axes[0])


def on_device(modes):
    width = modes.shape[2]
    blocks = lax.axis_size("blk")
    groups = lax.axis_size("res")
    devices = blocks * groups
    own = KEPT // groups
    device = lax.axis_index("res") * blocks + lax.axis_index("blk")
    first = PARTS * blocks
    mine = first // devices
    padded = first * width
    chunk = width // devices
    inner = 512
    outer = width // inner
    share = chunk // inner if chunk >= inner else 1
    low = chunk // share
    order = (own, groups, blocks)
    place = (iota(order, 1) * own + iota(order, 0)) * blocks + iota(order, 2)
    place = place.reshape(1, KEPT * blocks)
    forward = real_form(unit(iota((first, 1), 0) * place, first), 1.0)
    backward = real_form(unit(iota((first, 1), 0) * (place + SKIP * blocks), first), -1.0)
    row_u = iota((first, share), 0)
    row = unit(row_u * (device * chunk + low * iota((first, share), 1)), padded)
    col = unit(iota((first, low), 0) * iota((first, low), 1), padded)
    turn = cmul((row[0][:, :, None], row[1][:, :, None]), (col[0][:, None], col[1][:, None]))
    got = lax.all_to_all(
        modes.reshape(2, own, devices, share, low), AXES, split_axis=2, concat_axis=2, tiled=True
    )
    got = got.reshape(2, KEPT * blocks, share, low)
    section = jnp.einsum("aubm,bmxc->auxc", forward, got, precision=high)
    section = jnp.stack(cmul(turn, section))
    back = lax.all_to_all(
        section.reshape(2, devices, mine, share, low), AXES, split_axis=1, concat_axis=1, tiled=True
    )
    local = (
        back.reshape(2, devices, mine, chunk).transpose(0, 2, 1, 3).reshape(2, mine, outer, inner)
    )
    outer_pair = unit(iota((outer, outer), 0) * iota((outer, outer), 1), outer)
    inner_pair = unit(iota((inner, inner), 0) * iota((inner, inner), 1), inner)
    inner_turn = unit(iota((outer, inner), 0) * iota((outer, inner), 1), width)
    local = jnp.einsum("asbp,bxpc->axsc", real_form(outer_pair, 1.0), local, precision=high)
    local = jnp.stack(cmul(inner_turn, local))
    values = jnp.einsum("akbj,bxsj->axsk", real_form(inner_pair, 1.0), local, precision=high)
    squared = jnp.stack(
        [(values[0] - values[1]) * (values[0] + values[1]), 2.0 * values[0] * values[1]]
    )
    local = jnp.einsum("akbj,bxsj->axsk", real_form(inner_pair, -1.0), squared, precision=high)
    local = jnp.stack(cmul((inner_turn[0], -inner_turn[1]), local))
    local = jnp.einsum("asbp,bxpc->axsc", real_form(outer_pair, -1.0), local, precision=high)
    moved = lax.all_to_all(
        local.reshape(2, mine, devices, share, low).transpose(0, 2, 1, 3, 4),
        AXES,
        split_axis=1,
        concat_axis=1,
        tiled=True,
    )
    moved = moved.reshape(2, first, share, low)
    moved = jnp.stack(cmul((turn[0] * (1.0 / padded), turn[1] * (-1.0 / padded)), moved))
    result = jnp.einsum("aubm,buxc->amxc", backward, moved, precision=high)
    home = lax.all_to_all(
        result.reshape(2, own, devices, share, low), AXES, split_axis=2, concat_axis=2, tiled=True
    )
    return home.reshape(2, own, width)


def solution(mesh):
    return jax.shard_map(
        on_device,
        mesh=mesh,
        in_specs=(P(None, "res", "blk"),),
        out_specs=P(None, "res", "blk"),
        check_vma=False,
    )
```

profile of v0, /device:TPU:0, one launch (start us, length us, event | category | flops | bytes accessed | tf_op | source)
XLA Modules:
  0.0 1385.1 jit_solution(13819439389830380699)
XLA Ops:
  0.0 11.4 reshape.579
  11.4 15.4 %copy.42 = f32[2,2,32,32,512]{4,1,0,3,2:T(2,128)} copy(f32[2,2,32,32,512]{4,3,2,1,0:T(8,128)} %reshape.579) | data formatting | bytes 16777216 | tf_op jit(solution)/shard_map/reshape | solution.py:58
  26.8 7.6 all-to-all-start
  34.6 0.2 fusion.99
  34.8 0.3 copy-done.12
  35.1 0.8 fusion.71
  36.1 187.6 %all-to-all-done = f32[2,2,32,32,512]{4,1,0,3,2:T(2,128)} async-done(((f32[2,2,32,32,512]{4,1,0,3,2:T(2,128)}), f32[2,2,32,32,512]{4,1,0,3,2:T(2,128)}, u32[]{:S(2)}, u32[]{:S(2)}) %all-to-all-start) | async-done | bytes 8388640 | tf_op jit(solution)/shard_map/all_to_all | solution.py:57
  223.7 8.2 copy.43
  231.9 6.0 convolution_bitcast_fusion
  238.0 4.7 multiply_subtract_fusion.3
  242.7 6.4 copy.45
  249.1 6.3 copy.44
  255.4 9.5 pad_maximum_fusion
  265.0 12.0 copy.46
  277.0 4.2 all-to-all-start.1
  281.2 3.8 fusion.66
  285.0 4.1 fusion.64
  289.1 4.0 broadcast_multiply_fusion.1
  293.2 9.0 fusion.59
  302.2 8.6 fusion.62
  310.8 4.0 fusion.43
  314.8 16.5 %broadcast_multiply_fusion = (f32[1024,1,1024]{2,0,1:T(8,128)}, f32[1024,1,1024]{2,0,1:T(8,128)}) fusion(), kind=kLoop, calls=%fused_computation.81 | loop fusion | flops 15728640 | bytes 8388608 | tf_op jit(solution)/shard_map/mul | solution.py:29
  331.3 17.7 %fusion.48 = (f32[1024,1,1024]{2,0,1:T(8,128)}, f32[1024,1,1024]{2,0,1:T(8,128)}) fusion(), kind=kLoop, calls=%fused_computation.83 | loop fusion | flops 15728640 | bytes 8388608 | tf_op jit(solution)/shard_map/cos | solution.py:20
  348.9 16.3 %fusion.53 = f32[1024,1,1024]{2,0,1:T(8,128)} fusion(), kind=kLoop, calls=%fused_computation.88 | loop fusion | flops 16777216 | bytes 4194304 | tf_op jit(solution)/shard_map/neg | solution.py:30
  365.3 22.1 %fusion.20 = (f32[1,1024,2,1024]{3,1,2,0:T(8,128)}, f32[1,1024,2,1024]{3,1,2,0:T(8,128)}, f32[1,1024,2,1024]{3,1,2,0:T(8,128)}, f32[1,1024,2,1024]{3,1,2,0:T(8,128)}) fusion(f32[1024,1,1024]{2,0,1:T(8,128)} %get-tuple-element.39, f32[1024,1,1024]{2,0,1:T(8,128)} %get-tuple-element.40, f32[1024,1,1024]{2,0,1:T(8,128)} %get-tuple-element.37, ...), kind=kLoop, calls=%fused_computation.31 | loop fusion | flops 8388608 | bytes 54525952 | tf_op jit(solution)/shard_map/stack | solution.py:30
  387.3 175.9 %all-to-all-done.1 = f32[2,32,3,32,512]{4,3,2,0,1:T(8,128)} async-done(((f32[2,32,3,32,512]{4,3,2,0,1:T(8,128)}), f32[2,32,3,32,512]{4,3,2,0,1:T(8,128)}, u32[]{:S(2)}, u32[]{:S(2)}) %all-to-all-start.1) | async-done | bytes 12582944 | tf_op jit(solution)/shard_map/all_to_all | solution.py:63
  563.3 12.0 copy.47
  575.3 13.8 reshape.581
  589.1 13.8 reshape.582
  602.9 86.0 %fusion.24 = f32[2,3,1024,512]{2,3,0,1:T(8,128)} fusion(f32[1,1024,2,1024]{3,1,2,0:T(8,128)} %get-tuple-element.20, f32[1,1024,2,1024]{3,1,2,0:T(8,128)} %get-tuple-element.17, f32[2,3,1024,512]{3,2,1,0:T(8,128)} %reshape.582), kind=kOutput, calls=%fused_computation.50 | convolution fusion | flops 38658899968 | bytes 41943040 | tf_op jit(solution)/shard_map/asbp,bxpc->axsc/dot_general | solution.py:72
  688.9 5.7 multiply_subtract_fusion.2
  694.6 61.4 %fusion.28 = f32[2,3,1024,512]{3,2,0,1:T(8,128)S(1)} fusion(f32[1,3,1024,512]{2,3,0,1:T(8,128)S(1)} %get-tuple-element.8, f32[1,3,1024,512]{2,3,0,1:T(8,128)S(1)} %get-tuple-element.7, f32[1,512,2,512]{3,1,2,0:T(8,128)} %get-tuple-element.23, f32[1,512,2,512]{3,1,2,0:T(8,128)} %get-tuple-element.24), kind=kOutput, calls=%fused_computation.52 | convolution fusion | flops 19331547136 | bytes 29360128 | tf_op jit(solution)/shard_map/akbj,bxsj->axsk/dot_general | solution.py:74
  756.1 3.5 add_multiply_fusion
  759.6 24.9 %fusion.27 = f32[2,3,1024,512]{2,3,0,1:T(8,128)S(1)} fusion(f32[1,3,1024,512]{3,2,0,1:T(8,128)} %get-tuple-element.16, f32[1,3,1024,512]{3,2,0,1:T(8,128)S(1)} %get-tuple-element.15, f32[1,512,2,512]{3,1,2,0:T(8,128)} %get-tuple-element.22, f32[1,512,2,512]{3,1,2,0:T(8,128)} %get-tuple-element.21), kind=kOutput, calls=%fused_computation.51 | convolution fusion | flops 19331547136 | bytes 29360128 | tf_op jit(solution)/shard_map/akbj,bxsj->axsk/dot_general | solution.py:78
  784.5 5.9 multiply_subtract_fusion.1
  790.4 46.8 %fusion.29 = f32[2,3,1024,512]{2,3,0,1:T(8,128)} fusion(f32[1,1024,2,1024]{3,1,2,0:T(8,128)} %get-tuple-element.18, f32[1,1024,2,1024]{3,1,2,0:T(8,128)} %get-tuple-element.19, f32[1,3,1024,512]{2,3,0,1:T(8,128)} %get-tuple-element.6, f32[1,3,1024,512]{2,3,0,1:T(8,128)} %get-tuple-element.5), kind=kOutput, calls=%fused_computation.53 | convolution fusion | flops 38662045696 | bytes 41943040 | tf_op jit(solution)/shard_map/asbp,bxpc->axsc/dot_general | solution.py:80
  837.2 13.0 copy.51
  850.3 12.0 copy.52
  862.3 3.9 all-to-all-start.2
  866.5 0.7 maximum_bitcast_fusion.28
  867.2 281.6 %all-to-all-done.2 = f32[2,32,3,32,512]{4,3,2,0,1:T(8,128)} async-done(((f32[2,32,3,32,512]{4,3,2,0,1:T(8,128)}), f32[2,32,3,32,512]{4,3,2,0,1:T(8,128)}, u32[]{:S(2)}, u32[]{:S(2)}) %all-to-all-start.2) | async-done | bytes 12582944 | tf_op jit(solution)/shard_map/all_to_all | solution.py:81
  1148.7 9.5 fusion.106
  1158.3 9.6 multiply_subtract_fusion
  1167.9 5.7 fusion.14
  1173.6 8.1 copy.60
  1181.7 186.8 %all_to_all.20 = f32[2,2,32,32,512]{4,1,3,0,2:T(2,128)S(1)} all-to-all(f32[2,2,32,32,512]{4,1,3,0,2:T(2,128)S(1)} %copy.60), channel_id=1, replica_groups=mesh['res'=4,'blk'=8] {'res','blk'}, dimensions={2} | all-to-all | bytes 16777216 | tf_op jit(solution)/shard_map/all_to_all | solution.py:91
  1368.5 4.9 copy.61
  1373.4 11.4 reshape.585
  (35 shorter events, 0.6 us)
Async XLA Ops:
  26.8 196.9 %all-to-all-start = ((f32[2,2,32,32,512]{4,1,0,3,2:T(2,128)}), f32[2,2,32,32,512]{4,1,0,3,2:T(2,128)}, u32[]{:S(2)}, u32[]{:S(2)}) async-start(f32[2,2,32,32,512]{4,1,0,3,2:T(2,128)} %copy.42), calls=%async_computation | async-start | bytes 16777216 | tf_op jit(solution)/shard_map/all_to_all | solution.py:57
  34.6 0.5 copy-start.12
  35.9 202.0 %copy-start.2 = (f32[96,512]{1,0:T(8,128)}, f32[96,512]{1,0:T(8,128)S(1)}, u32[]{:S(2)}) copy-start(f32[96,512]{1,0:T(8,128)S(1)} %get-tuple-element.41) | copy-start | bytes 589828
  35.9 202.0 %copy-start.4 = (f32[96,512]{1,0:T(8,128)}, f32[96,512]{1,0:T(8,128)S(1)}, u32[]{:S(2)}) copy-start(f32[96,512]{1,0:T(8,128)S(1)} %get-tuple-element.42) | copy-start | bytes 589828
  36.1 201.9 %copy-start.8 = (f32[96,32]{0,1:T(8,128)}, f32[96,32]{0,1:T(8,128)S(1)}, u32[]{:S(2)}) copy-start(f32[96,32]{0,1:T(8,128)S(1)} %get-tuple-element.32) | copy-start | bytes 36868
  36.1 201.9 %copy-start.10 = (f32[96,32]{0,1:T(8,128)}, f32[96,32]{0,1:T(8,128)S(1)}, u32[]{:S(2)}) copy-start(f32[96,32]{0,1:T(8,128)S(1)} %get-tuple-element.33) | copy-start | bytes 36868
  277.0 286.3 %all-to-all-start.1 = ((f32[2,32,3,32,512]{4,3,2,0,1:T(8,128)}), f32[2,32,3,32,512]{4,3,2,0,1:T(8,128)}, u32[]{:S(2)}, u32[]{:S(2)}) async-start(f32[2,32,3,32,512]{4,3,2,0,1:T(8,128)} %copy.46), calls=%async_computation.1 | async-start | bytes 25165824 | tf_op jit(solution)/shard_map/all_to_all | solution.py:63
  602.9 86.0 %copy-start.1 = (f32[1024,512]{0,1:T(8,128)S(1)}, f32[1024,512]{0,1:T(8,128)}, u32[]{:S(2)}) copy-start(f32[1024,512]{0,1:T(8,128)} %get-tuple-element.43) | copy-start | bytes 6291460
  759.6 24.9 %copy-start = (f32[1024,512]{0,1:T(8,128)S(1)}, f32[1024,512]{0,1:T(8,128)}, u32[]{:S(2)}) copy-start(f32[1024,512]{0,1:T(8,128)} %fusion.62) | copy-start | bytes 6291460
  862.3 3.9 copy-start.13
  862.3 286.4 %all-to-all-start.2 = ((f32[2,32,3,32,512]{4,3,2,0,1:T(8,128)}), f32[2,32,3,32,512]{4,3,2,0,1:T(8,128)}, u32[]{:S(2)}, u32[]{:S(2)}) async-start(f32[2,32,3,32,512]{4,3,2,0,1:T(8,128)} %copy.52), calls=%async_computation.2 | async-start | bytes 25165824 | tf_op jit(solution)/shard_map/all_to_all | solution.py:81
  867.2 291.1 %copy-start.3 = (f32[96,512]{1,0:T(8,128)S(1)}, f32[96,512]{1,0:T(8,128)}, u32[]{:S(2)}) copy-start(f32[96,512]{1,0:T(8,128)} %copy-done.2) | copy-start | bytes 589828
  867.2 291.1 %copy-start.5 = (f32[96,512]{1,0:T(8,128)S(1)}, f32[96,512]{1,0:T(8,128)}, u32[]{:S(2)}) copy-start(f32[96,512]{1,0:T(8,128)} %copy-done.4) | copy-start | bytes 589828
  867.2 291.1 %copy-start.9 = (f32[96,32]{0,1:T(8,128)S(1)}, f32[96,32]{0,1:T(8,128)}, u32[]{:S(2)}) copy-start(f32[96,32]{0,1:T(8,128)} %copy-done.8) | copy-start | bytes 36868
  867.2 291.1 %copy-start.11 = (f32[96,32]{0,1:T(8,128)S(1)}, f32[96,32]{0,1:T(8,128)}, u32[]{:S(2)}) copy-start(f32[96,32]{0,1:T(8,128)} %copy-done.10) | copy-start | bytes 36868
  1158.3 9.6 copy-start.6
  1158.3 9.6 copy-start.7
where the time goes:
time: 1390 us
  waiting for transfers between devices  645 us (46%)
  matrix products  231 us (17%)
  blocking collectives  187 us (13%)
  local copies, waits for them, and re-layouts  159 us (11%)
  other arithmetic  147 us (11%)
  starting transfers between devices  15.7 us (1%)
    all_to_all x1, waiting for transfers between devices, on_device(): lax.all_to_all(local.reshape(2, mine, devices, share, low).transpose(0, 2...  282 us
    all_to_all x1, waiting for transfers between devices, on_device(): lax.all_to_all(modes.reshape(2, own, devices, share, low), AXES, split_ax...  188 us
    all_to_all x1, blocking collectives, on_device(): lax.all_to_all(result.reshape(2, own, devices, share, low), AXES, split_a...  187 us
    all_to_all x1, waiting for transfers between devices, on_device(): lax.all_to_all(section.reshape(2, devices, mine, share, low), AXES, split...  176 us
    dot_general x1, matrix products, on_device(): jnp.einsum('asbp,bxpc->axsc', real_form(outer_pair, 1.0), local, precisio...  86 us
    dot_general x1, matrix products, on_device(): jnp.einsum('akbj,bxsj->axsk', real_form(inner_pair, 1.0), local, precisio...  61.4 us
    dot_general x1, matrix products, on_device(): jnp.einsum('asbp,bxpc->axsc', real_form(outer_pair, -1.0), local, precisi...  46.8 us
  transfers between devices with their start and end apart: 3, of which 3 were waited for; matrix products, arithmetic and copies ran while one was open for 8% of the time, Pallas kernels for 0%

commit v1 on v0

--- a/solution.py
+++ b/solution.py
@@ -78,13 +78,11 @@
     local = jnp.einsum("akbj,bxsj->axsk", real_form(inner_pair, -1.0), squared, precision=high)
     local = jnp.stack(cmul((inner_turn[0], -inner_turn[1]), local))
     local = jnp.einsum("asbp,bxpc->axsc", real_form(outer_pair, -1.0), local, precision=high)
-    moved = lax.all_to_all(
-        local.reshape(2, mine, devices, share, low).transpose(0, 2, 1, 3, 4),
-        AXES,
-        split_axis=1,
-        concat_axis=1,
-        tiled=True,
-    )
+    block = local.reshape(2, mine, devices, share, low).transpose(0, 2, 1, 3, 4)
+    size = lax.axis_size(AXES)
+    pieces = jnp.stack(jnp.split(block, size, axis=1), axis=0)
+    pieces = lax.all_to_all(pieces, AXES, split_axis=0, concat_axis=0)
+    moved = jnp.concatenate(pieces, axis=1)
     moved = moved.reshape(2, first, share, low)
     moved = jnp.stack(cmul((turn[0] * (1.0 / padded), turn[1] * (-1.0 / padded)), moved))
     result = jnp.einsum("aubm,buxc->amxc", backward, moved, precision=high)

time: 1390 us -> 1420 us (1.022)
  local copies, waits for them, and re-layouts: 159 us -> 189 us
    unnamed x28 -> x61, local copies, waits for them, and re-layouts: 0.31 us -> 41.6 us
where the time goes in v1:
time: 1420 us
  waiting for transfers between devices  645 us (45%)
  matrix products  231 us (16%)
  local copies, waits for them, and re-layouts  189 us (13%)
  blocking collectives  187 us (13%)
  other arithmetic  147 us (10%)
  starting transfers between devices  15.7 us (1%)
    all_to_all x1, waiting for transfers between devices, on_device(): pieces = lax.all_to_all(pieces, AXES, split_axis=0, concat_axis=0)  282 us
    all_to_all x1, waiting for transfers between devices, on_device(): lax.all_to_all(modes.reshape(2, own, devices, share, low), AXES, split_ax...  188 us
    all_to_all x1, blocking collectives, on_device(): lax.all_to_all(result.reshape(2, own, devices, share, low), AXES, split_a...  187 us
    all_to_all x1, waiting for transfers between devices, on_device(): lax.all_to_all(section.reshape(2, devices, mine, share, low), AXES, split...  176 us
    dot_general x1, matrix products, on_device(): jnp.einsum('asbp,bxpc->axsc', real_form(outer_pair, 1.0), local, precisio...  86 us
    dot_general x1, matrix products, on_device(): jnp.einsum('akbj,bxsj->axsk', real_form(inner_pair, 1.0), local, precisio...  61.4 us
    dot_general x1, matrix products, on_device(): jnp.einsum('asbp,bxpc->axsc', real_form(outer_pair, -1.0), local, precisi...  46.9 us
    unnamed x61, local copies, waits for them, and re-layouts  41.6 us
  transfers between devices with their start and end apart: 3, of which 3 were waited for; matrix products, arithmetic and copies ran while one was open for 8% of the time, Pallas kernels for 0%

profile of v1, /device:TPU:0, one launch (start us, length us, event | category | flops | bytes accessed | tf_op | source)
XLA Modules:
  0.0 1415.1 jit_solution(15624388754371056514)
XLA Ops:
  0.0 11.4 reshape.581
  11.4 15.4 %copy.130 = f32[2,2,32,32,512]{4,1,0,3,2:T(2,128)} copy(f32[2,2,32,32,512]{4,3,2,1,0:T(8,128)} %reshape.581) | data formatting | bytes 16777216 | tf_op jit(solution)/shard_map/reshape | solution.py:58
  26.8 7.6 all-to-all-start
  36.1 187.5 %all-to-all-done = f32[2,2,32,32,512]{4,1,0,3,2:T(2,128)} async-done(((f32[2,2,32,32,512]{4,1,0,3,2:T(2,128)}), f32[2,2,32,32,512]{4,1,0,3,2:T(2,128)}, u32[]{:S(2)}, u32[]{:S(2)}) %all-to-all-start) | async-done | bytes 8388640 | tf_op jit(solution)/shard_map/all_to_all | solution.py:57
  223.7 8.2 copy.131
  231.9 6.0 convolution_bitcast_fusion
  238.0 4.7 multiply_subtract_fusion.3
  242.7 6.4 copy.133
  249.1 6.3 copy.132
  255.4 9.5 pad_maximum_fusion
  265.0 12.1 copy.134
  277.0 4.2 all-to-all-start.1
  281.2 3.8 fusion.66
  285.0 4.1 fusion.64
  289.2 4.0 broadcast_multiply_fusion.1
  293.2 9.0 fusion.59
  302.2 8.6 fusion.62
  310.8 4.0 fusion.43
  314.8 16.5 %broadcast_multiply_fusion = (f32[1024,1,1024]{2,0,1:T(8,128)}, f32[1024,1,1024]{2,0,1:T(8,128)}) fusion(), kind=kLoop, calls=%fused_computation.81 | loop fusion | flops 15728640 | bytes 8388608 | tf_op jit(solution)/shard_map/mul | solution.py:29
  331.3 17.7 %fusion.48 = (f32[1024,1,1024]{2,0,1:T(8,128)}, f32[1024,1,1024]{2,0,1:T(8,128)}) fusion(), kind=kLoop, calls=%fused_computation.83 | loop fusion | flops 15728640 | bytes 8388608 | tf_op jit(solution)/shard_map/cos | solution.py:20
  348.9 16.3 %fusion.53 = f32[1024,1,1024]{2,0,1:T(8,128)} fusion(), kind=kLoop, calls=%fused_computation.88 | loop fusion | flops 16777216 | bytes 4194304 | tf_op jit(solution)/shard_map/neg | solution.py:30
  365.3 22.1 %fusion.20 = (f32[1,1024,2,1024]{3,1,2,0:T(8,128)}, f32[1,1024,2,1024]{3,1,2,0:T(8,128)}, f32[1,1024,2,1024]{3,1,2,0:T(8,128)}, f32[1,1024,2,1024]{3,1,2,0:T(8,128)}) fusion(f32[1024,1,1024]{2,0,1:T(8,128)} %get-tuple-element.39, f32[1024,1,1024]{2,0,1:T(8,128)} %get-tuple-element.40, f32[1024,1,1024]{2,0,1:T(8,128)} %get-tuple-element.37, ...), kind=kLoop, calls=%fused_computation.31 | loop fusion | flops 8388608 | bytes 54525952 | tf_op jit(solution)/shard_map/stack | solution.py:30
  387.4 175.9 %all-to-all-done.1 = f32[2,32,3,32,512]{4,3,2,0,1:T(8,128)} async-done(((f32[2,32,3,32,512]{4,3,2,0,1:T(8,128)}), f32[2,32,3,32,512]{4,3,2,0,1:T(8,128)}, u32[]{:S(2)}, u32[]{:S(2)}) %all-to-all-start.1) | async-done | bytes 12582944 | tf_op jit(solution)/shard_map/all_to_all | solution.py:63
  563.3 12.1 copy.135
  575.4 13.8 reshape.583
  589.1 13.8 reshape.584
  603.0 86.0 %fusion.24 = f32[2,3,1024,512]{2,3,0,1:T(8,128)} fusion(f32[1,1024,2,1024]{3,1,2,0:T(8,128)} %get-tuple-element.20, f32[1,1024,2,1024]{3,1,2,0:T(8,128)} %get-tuple-element.17, f32[2,3,1024,512]{3,2,1,0:T(8,128)} %reshape.584), kind=kOutput, calls=%fused_computation.50 | convolution fusion | flops 38658899968 | bytes 41943040 | tf_op jit(solution)/shard_map/asbp,bxpc->axsc/dot_general | solution.py:72
  689.0 5.7 multiply_subtract_fusion.2
  694.7 61.4 %fusion.28 = f32[2,3,1024,512]{3,2,0,1:T(8,128)S(1)} fusion(f32[1,3,1024,512]{2,3,0,1:T(8,128)S(1)} %get-tuple-element.8, f32[1,3,1024,512]{2,3,0,1:T(8,128)S(1)} %get-tuple-element.7, f32[1,512,2,512]{3,1,2,0:T(8,128)} %get-tuple-element.23, f32[1,512,2,512]{3,1,2,0:T(8,128)} %get-tuple-element.24), kind=kOutput, calls=%fused_computation.52 | convolution fusion | flops 19331547136 | bytes 29360128 | tf_op jit(solution)/shard_map/akbj,bxsj->axsk/dot_general | solution.py:74
  756.1 3.5 add_multiply_fusion
  759.7 24.9 %fusion.27 = f32[2,3,1024,512]{2,3,0,1:T(8,128)S(1)} fusion(f32[1,3,1024,512]{3,2,0,1:T(8,128)} %get-tuple-element.16, f32[1,3,1024,512]{3,2,0,1:T(8,128)S(1)} %get-tuple-element.15, f32[1,512,2,512]{3,1,2,0:T(8,128)} %get-tuple-element.22, f32[1,512,2,512]{3,1,2,0:T(8,128)} %get-tuple-element.21), kind=kOutput, calls=%fused_computation.51 | convolution fusion | flops 19331547136 | bytes 29360128 | tf_op jit(solution)/shard_map/akbj,bxsj->axsk/dot_general | solution.py:78
  784.6 5.9 multiply_subtract_fusion.1
  790.5 46.9 %fusion.29 = f32[2,3,1024,512]{2,3,0,1:T(8,128)} fusion(f32[1,1024,2,1024]{3,1,2,0:T(8,128)} %get-tuple-element.18, f32[1,1024,2,1024]{3,1,2,0:T(8,128)} %get-tuple-element.19, f32[1,3,1024,512]{2,3,0,1:T(8,128)} %get-tuple-element.6, f32[1,3,1024,512]{2,3,0,1:T(8,128)} %get-tuple-element.5), kind=kOutput, calls=%fused_computation.53 | convolution fusion | flops 38662045696 | bytes 41943040 | tf_op jit(solution)/shard_map/asbp,bxpc->axsc/dot_general | solution.py:80
  837.3 12.9 copy.139
  850.3 2.0 fusion.98
  852.2 2.5 fusion.97
  858.2 1.8 fusion.94
  861.8 1.8 fusion.92
  872.5 1.8 fusion.86
  892.3 3.9 all-to-all-start.2
  897.1 281.6 %all-to-all-done.2 = f32[32,2,1,3,32,512]{5,4,3,1,2,0:T(8,128)} async-done(((f32[32,2,1,3,32,512]{5,4,3,1,2,0:T(8,128)}), f32[32,2,1,3,32,512]{5,4,3,1,2,0:T(8,128)}, u32[]{:S(2)}, u32[]{:S(2)}) %all-to-all-start.2) | async-done | bytes 12582944 | tf_op jit(solution)/shard_map/all_to_all | solution.py:84
  1178.7 9.6 fusion.138
  1188.3 9.6 multiply_subtract_fusion
  1197.9 5.7 fusion.14
  1203.6 8.1 copy.176
  1211.7 186.8 %all_to_all.20 = f32[2,2,32,32,512]{4,1,3,0,2:T(2,128)S(1)} all-to-all(f32[2,2,32,32,512]{4,1,3,0,2:T(2,128)S(1)} %copy.176), channel_id=1, replica_groups=mesh['res'=4,'blk'=8] {'res','blk'}, dimensions={2} | all-to-all | bytes 16777216 | tf_op jit(solution)/shard_map/all_to_all | solution.py:89
  1398.5 4.9 copy.177
  1403.4 11.4 reshape.588
  (68 shorter events, 34.8 us)
Async XLA Ops:
  26.8 196.9 %all-to-all-start = ((f32[2,2,32,32,512]{4,1,0,3,2:T(2,128)}), f32[2,2,32,32,512]{4,1,0,3,2:T(2,128)}, u32[]{:S(2)}, u32[]{:S(2)}) async-start(f32[2,2,32,32,512]{4,1,0,3,2:T(2,128)} %copy.130), calls=%async_computation | async-start | bytes 16777216 | tf_op jit(solution)/shard_map/all_to_all | solution.py:57
  34.6 0.5 copy-start.13
  35.9 202.0 %copy-start.3 = (f32[96,512]{1,0:T(8,128)}, f32[96,512]{1,0:T(8,128)S(1)}, u32[]{:S(2)}) copy-start(f32[96,512]{1,0:T(8,128)S(1)} %get-tuple-element.41) | copy-start | bytes 589828
  35.9 202.0 %copy-start.5 = (f32[96,512]{1,0:T(8,128)}, f32[96,512]{1,0:T(8,128)S(1)}, u32[]{:S(2)}) copy-start(f32[96,512]{1,0:T(8,128)S(1)} %get-tuple-element.42) | copy-start | bytes 589828
  36.1 201.8 %copy-start.9 = (f32[96,32]{0,1:T(8,128)}, f32[96,32]{0,1:T(8,128)S(1)}, u32[]{:S(2)}) copy-start(f32[96,32]{0,1:T(8,128)S(1)} %get-tuple-element.32) | copy-start | bytes 36868
  36.1 201.8 %copy-start.11 = (f32[96,32]{0,1:T(8,128)}, f32[96,32]{0,1:T(8,128)S(1)}, u32[]{:S(2)}) copy-start(f32[96,32]{0,1:T(8,128)S(1)} %get-tuple-element.33) | copy-start | bytes 36868
  277.0 286.3 %all-to-all-start.1 = ((f32[2,32,3,32,512]{4,3,2,0,1:T(8,128)}), f32[2,32,3,32,512]{4,3,2,0,1:T(8,128)}, u32[]{:S(2)}, u32[]{:S(2)}) async-start(f32[2,32,3,32,512]{4,3,2,0,1:T(8,128)} %copy.134), calls=%async_computation.1 | async-start | bytes 25165824 | tf_op jit(solution)/shard_map/all_to_all | solution.py:63
  603.0 86.0 %copy-start.2 = (f32[1024,512]{0,1:T(8,128)S(1)}, f32[1024,512]{0,1:T(8,128)}, u32[]{:S(2)}) copy-start(f32[1024,512]{0,1:T(8,128)} %get-tuple-element.43) | copy-start | bytes 6291460
  759.6 24.9 %copy-start.1 = (f32[1024,512]{0,1:T(8,128)S(1)}, f32[1024,512]{0,1:T(8,128)}, u32[]{:S(2)}) copy-start(f32[1024,512]{0,1:T(8,128)} %fusion.62) | copy-start | bytes 6291460
  850.2 29.4 %copy-start = (f32[2,3,1024,512]{3,2,1,0:T(8,128)S(1)}, f32[2,3,1024,512]{3,2,1,0:T(8,128)}, u32[]{:S(2)}) copy-start(f32[2,3,1024,512]{3,2,1,0:T(8,128)} %copy.139) | copy-start | bytes 37748740
  892.3 3.9 copy-start.14
  892.3 286.4 %all-to-all-start.2 = ((f32[32,2,1,3,32,512]{5,4,3,1,2,0:T(8,128)}), f32[32,2,1,3,32,512]{5,4,3,1,2,0:T(8,128)}, u32[]{:S(2)}, u32[]{:S(2)}) async-start(f32[32,2,1,3,32,512]{5,4,3,1,2,0:T(8,128)} %fusion.67), calls=%async_computation.2 | async-start | bytes 25165824 | tf_op jit(solution)/shard_map/all_to_all | solution.py:84
  1178.7 9.6 copy-start.4
  1178.7 9.6 copy-start.6
  1178.7 9.6 copy-start.10
  1178.7 9.6 copy-start.12
  1188.3 9.6 copy-start.7
  1188.3 9.6 copy-start.8
